TPU v7x, 32 devices: a whole 2x2x4 slice. The times are simulated.
32 devices in a mesh: blk: 8 (over y, x, core), pitch: 4 (over z).
Axes of the slice: x: 2, y: 2, z: 4, core: 2. Of those that a mesh axis runs over, the one named last changes fastest.
Arguments:
- flow_state: float32 [5, 32, 128, 128], P(None, 'pitch', 'blk'), may hold values from -0.6 to 3.2, as said below
- prior_state: float32 [5, 32, 128, 128], P(None, 'pitch', 'blk'), may hold values from -0.75 to 3.35, as said below
- fourier_store: float32 [2, 49, 10, 128, 128], P(None, None, None, ('blk', 'pitch')), may hold values from -0.15 to 2.6, as said below
- sample_times: int32 [2, 128, 128], P(None, ('blk', 'pitch')), may hold values from 0 to 95
- harmonics: int32 [128, 128], P(('blk', 'pitch')), may hold values from 12 to 24
Outputs:
- new_state: float32 [5, 32, 128, 128], P(None, 'pitch', 'blk')
- new_store: float32 [2, 49, 10, 128, 128], P(None, None, None, ('blk', 'pitch'))
- new_ghosts: float32 [2, 10, 128, 128], P(None, None, ('blk', 'pitch'))
Inputs may be any that keep to these rules, and one draw needn't show every extreme that they name: `flow_state`: density between 0.7 and 1.3, momenta between -0.6 and 0.6, total energy between 2.2 and 3.2. `prior_state`: each entry within 0.15 of flow_state's. `fourier_store`: the k-th cosine and sine coefficients are at most 0.08 / k in magnitude.
All inputs are finite; a program needn't handle non-finite values.
Results may differ from a plain program's by a relative error of at most 0.000068.
Values sent between devices are 32-bit elements; how exact they have to be, the bound alone decides.
No kernel may reach another device: no remote copies, remote signals or barrier semaphores. Data moves between devices by JAX's collectives and lax.ppermute only.
A program may use at most 64 MiB of HBM per device.

v0:
```python
import math
import jax
import jax.numpy as jnp
from jax import lax
from jax.sharding import PartitionSpec as P

NT = 96
gamma_less = 0.4
diss_coeff = 0.03125
section_coefs = (1.0 / 3.0, 0.5, 1.0)
pseudo_step = 0.1
physical_step = 0.25
relax_rate = 0.125
lag_turns = 0.3


def padded_2(block, sides, width):
    for axis, dim in sides:
        count = lax.axis_size(axis)
        forward = [(i, i + 1) for i in range(count - 1)]
        backward = [(target, source) for source, target in forward]
        low = lax.ppermute(
            lax.slice_in_dim(block, block.shape[dim] - width, None, axis=dim), axis, forward
        )
        high = lax.ppermute(lax.slice_in_dim(block, 0, width, axis=dim), axis, backward)
        block = jnp.concatenate([low, block, high], axis=dim)
    return block


def fluxes(current, direction):
    density = current[0]
    velocity = current[direction] / density
    pressure = gamma_less * (
        current[4]
        - 0.5
        * (current[1] * current[1] + current[2] * current[2] + current[3] * current[3])
        / density
    )
    flux_parts = [
        current[direction],
        current[1] * velocity,
        current[2] * velocity,
        current[3] * velocity,
        (current[4] + pressure) * velocity,
    ]
    flux_parts[direction] = flux_parts[direction] + pressure
    return jnp.stack(flux_parts)


def face_sum(padded, direction):
    cells_n = padded.shape[direction] - 4
    faces_n = cells_n + 1
    cell_flux = fluxes(padded, direction)

    def window(values, offset, length):
        return lax.slice_in_dim(values, offset, offset + length, axis=direction)

    face_flux = 0.5 * (
        window(cell_flux, 1, faces_n) + window(cell_flux, 2, faces_n)
    ) - diss_coeff * (
        window(padded, 3, faces_n)
        - 3.0 * window(padded, 2, faces_n)
        + 3.0 * window(padded, 1, faces_n)
        - window(padded, 0, faces_n)
    )
    return window(face_flux, 1, cells_n) - window(face_flux, 0, cells_n)


def harmonic_tables(phases_at, harm_count):
    orders = jnp.arange(1, harm_count + 1).astype(jnp.float32).reshape((harm_count, 1, 1))
    angles = orders * phases_at[None]
    return (jnp.cos(angles), jnp.sin(angles))


def rebuild(coeffs, phases_at, active):
    harm_count = (coeffs.shape[0] - 1) // 2
    cosines, sines = harmonic_tables(phases_at, harm_count)
    orders = jnp.arange(1, harm_count + 1).reshape((harm_count, 1, 1))
    active_mask = (orders <= active[None]).astype(jnp.float32)
    harm_terms = (
        coeffs[1 : harm_count + 1] * (active_mask * cosines)[:, None]
        + coeffs[harm_count + 1 :] * (active_mask * sines)[:, None]
    )
    return coeffs[0] + jnp.sum(harm_terms, axis=0)


def refresh(coeffs, samples, phases_at):
    harm_count = (coeffs.shape[0] - 1) // 2
    cosines, sines = harmonic_tables(phases_at, harm_count)
    mean_part = (1.0 - relax_rate) * coeffs[0] + relax_rate * samples
    cos_part = (1.0 - relax_rate) * coeffs[1 : harm_count + 1] + 2.0 * relax_rate * samples[
        None
    ] * cosines[:, None]
    sin_part = (1.0 - relax_rate) * coeffs[harm_count + 1 :] + 2.0 * relax_rate * samples[
        None
    ] * sines[:, None]
    return jnp.concatenate([mean_part[None], cos_part, sin_part], axis=0)


def shards(flow_state, prior_state, fourier_store, sample_times, harmonics):
    pitch_at = lax.axis_index("pitch")
    pitch_end = lax.axis_size("pitch") - 1
    blk_at = lax.axis_index("blk")
    blk_end = lax.axis_size("blk") - 1
    block_rows = flow_state.shape[2]
    radial_cells = flow_state.shape[3]
    period = 2.0 * math.pi / NT
    phase_lag = 2.0 * math.pi * lag_turns
    phases = sample_times.astype(jnp.float32) * period
    low_share = rebuild(fourier_store[0], phases[0] - phase_lag, harmonics)
    high_share = rebuild(fourier_store[1], phases[1] + phase_lag, harmonics)
    low_whole, high_whole = (
        lax.all_gather(low_share, "pitch", axis=1, tiled=True),
        lax.all_gather(high_share, "pitch", axis=1, tiled=True),
    )
    ghost_shape = (5, 2, block_rows, radial_cells)
    low_ghost = low_whole.reshape(ghost_shape)
    high_ghost = high_whole.reshape(ghost_shape)
    current = flow_state
    for section_coef in section_coefs:
        pitch_pad = padded_2(current, (("pitch", 1),), 2)
        axial_pad = padded_2(current, (("blk", 2),), 2)
        pitch_pad = jnp.concatenate(
            [
                jnp.where(pitch_at == 0, low_ghost, pitch_pad[:, :2]),
                current,
                jnp.where(pitch_at == pitch_end, high_ghost, pitch_pad[:, -2:]),
            ],
            axis=1,
        )
        lower_edge = jnp.broadcast_to(current[:, :, :1], axial_pad[:, :, :2].shape)
        upper_edge = jnp.broadcast_to(current[:, :, -1:], axial_pad[:, :, :2].shape)
        axial_pad = jnp.concatenate(
            [
                jnp.where(blk_at == 0, lower_edge, axial_pad[:, :, :2]),
                current,
                jnp.where(blk_at == blk_end, upper_edge, axial_pad[:, :, -2:]),
            ],
            axis=2,
        )
        radial_pad = jnp.pad(current, ((0, 0), (0, 0), (0, 0), (2, 2)), mode="edge")
        summed = face_sum(pitch_pad, 1) + face_sum(axial_pad, 2) + face_sum(radial_pad, 3)
        summed = summed + (3.0 * current - 4.0 * flow_state + prior_state) * (0.5 / physical_step)
        current = flow_state - section_coef * pseudo_step * summed
    face_shape = (10, block_rows, radial_cells)
    upper_face = current[:, -2:].reshape(face_shape)
    lower_face = current[:, :2].reshape(face_shape)
    nothing = jnp.zeros_like(lower_face)
    upper_mine, lower_mine = (
        lax.psum_scatter(
            jnp.where(pitch_at == pitch_end, upper_face, nothing),
            "pitch",
            scatter_dimension=1,
            tiled=True,
        ),
        lax.psum_scatter(
            jnp.where(pitch_at == 0, lower_face, nothing), "pitch", scatter_dimension=1, tiled=True
        ),
    )
    next_phases = phases + period
    low_store = refresh(fourier_store[0], upper_mine, next_phases[0])
    high_store = refresh(fourier_store[1], lower_mine, next_phases[1])
    ghosts = jnp.stack(
        [
            rebuild(low_store, next_phases[0] - phase_lag, harmonics),
            rebuild(high_store, next_phases[1] + phase_lag, harmonics),
        ]
    )
    return (current, jnp.stack([low_store, high_store]), ghosts)


def solution(mesh):
    placed = (
        P(None, "pitch", "blk", None),
        P(None, "pitch", "blk", None),
        P(None, None, None, ("blk", "pitch"), None),
        P(None, ("blk", "pitch"), None),
        P(("blk", "pitch"), None),
    )
    return jax.shard_map(
        shards,
        mesh=mesh,
        in_specs=placed,
        out_specs=(
            P(None, "pitch", "blk", None),
            P(None, None, None, ("blk", "pitch"), None),
            P(None, None, ("blk", "pitch"), None),
        ),
        check_vma=False,
    )
```

profile of v0, /device:TPU:0, one launch (start us, length us, event | category | flops | bytes accessed | tf_op | source)
XLA Modules:
  0.0 152.5 jit_solution(4150837358878901428)
XLA Ops:
  7.2 1.7 %fusion.114 = (f32[5,8,2,128]{3,2,1,0:T(2,128)}, f32[5,8,2,128]{3,2,1,0:T(2,128)}) fusion(f32[5,8,16,128]{3,2,1,0:T(8,128)} %param.5), kind=kLoop, calls=%fused_computation.305 | loop fusion | bytes 163840 | tf_op jit(solution)/shard_map/slice | solution.py:25
  8.9 3.0 %collective-permute-start.2 = (f32[5,8,2,128]{3,2,1,0:T(2,128)}, f32[5,8,2,128]{3,2,1,0:T(2,128)}, u32[]{:S(2)}, u32[]{:S(2)}) collective-permute-start(f32[5,8,2,128]{3,2,1,0:T(2,128)} %get-tuple-element.86), channel_id=1, source_target_pairs={{0,4},{4,8},{8,12},{12,16},{16,20},{20,24},{24,28},{1,5},{5,9},{9,... | collective-permute-start | bytes 122888 | tf_op jit(solution)/shard_map/ppermute | solution.py:22
  11.9 1.3 collective-permute-start.3
  13.2 1.6 %fusion.112 = (f32[5,2,16,128]{3,2,1,0:T(8,128)}, f32[5,2,16,128]{3,2,1,0:T(8,128)}) fusion(f32[5,8,16,128]{3,2,1,0:T(8,128)} %param.5), kind=kLoop, calls=%fused_computation.303 | loop fusion | bytes 327680 | tf_op jit(solution)/shard_map/slice | solution.py:25
  14.8 4.9 %collective-permute-start = (f32[5,2,16,128]{3,2,1,0:T(8,128)}, f32[5,2,16,128]{3,2,1,0:T(8,128)}, u32[]{:S(2)}, u32[]{:S(2)}) collective-permute-start(f32[5,2,16,128]{3,2,1,0:T(8,128)} %get-tuple-element.82), channel_id=1, source_target_pairs={{0,1},{1,2},{2,3},{4,5},{5,6},{6,7},{8,9},{9,10},{10,11},{12,13},{... | collective-permute-start | bytes 245768 | tf_op jit(solution)/shard_map/ppermute | solution.py:22
  19.7 1.3 collective-permute-start.1
  21.0 1.2 fusion.115
  22.2 1.6 %fusion.113 = (f32[5,8,1,128]{3,2,1,0:T(1,128)}, f32[5,8,1,128]{3,2,1,0:T(1,128)}) fusion(f32[5,8,16,128]{3,2,1,0:T(8,128)} %param.5), kind=kLoop, calls=%fused_computation.304 | loop fusion | bytes 81920 | tf_op jit(solution)/shard_map/slice | solution.py:132
  23.9 0.3 copy.62
  24.2 0.3 copy.63
  24.5 0.2 reshape.105
  24.7 0.1 reshape.106
  24.8 0.3 pad_maximum_fusion.7
  25.4 1.1 fusion.16
  26.5 2.9 %multiply_sine_fusion.3 = (f32[24,4,128]{2,1,0:T(4,128)S(1)}, f32[24,4,128]{2,1,0:T(4,128)S(1)}, f32[24,4,128]{2,1,0:T(4,128)S(1)}, f32[24,4,128]{2,1,0:T(4,128)...) fusion(f32[4,128]{1,0:T(4,128)S(1)} %get-tuple-element.128, ...), kind=kLoop, calls=%fused_computation.246 | loop fusion | flops 184320 | bytes 604352 | tf_op jit(solution)/shard_map/sin | solution.py:72
  29.4 0.4 fusion.43
  29.8 0.6 bitcast_add_fusion
  30.5 14.3 %all_gather.6 = f32[10,16,128]{2,0,1:T(8,128)S(1)} all-gather(f32[10,4,128]{2,0,1:T(8,128)S(1)} %copy.52), channel_id=1, replica_groups=mesh['blk'=8,'pitch'=4] {'pitch'}, dimensions={1}, use_global_device_ids=true | all-gather | bytes 102400 | tf_op jit(solution)/shard_map/all_gather | solution.py:113
  44.8 0.7 copy.54
  45.6 13.3 %all_gather.7 = f32[10,16,128]{2,0,1:T(8,128)S(1)} all-gather(f32[10,4,128]{2,0,1:T(8,128)S(1)} %copy.54), channel_id=1, replica_groups=mesh['blk'=8,'pitch'=4] {'pitch'}, dimensions={1}, use_global_device_ids=true | all-gather | bytes 102400 | tf_op jit(solution)/shard_map/all_gather | solution.py:114
  59.0 0.8 broadcast_select_fusion.5
  59.7 0.8 broadcast_select_fusion.2
  60.8 0.4 fusion.37
  61.2 0.9 broadcast_select_fusion.8
  62.3 0.1 fusion.71
  62.5 0.7 copy-done.2
  63.2 0.2 fusion.93
  63.4 0.4 slice_reduce_fusion.2
  63.8 0.1 reshape.107
  64.0 0.1 reshape.108
  64.1 0.3 pad_maximum_fusion.8
  64.7 1.1 fusion.9
  65.8 1.3 collective-permute-start.6
  67.1 1.3 collective-permute-start.7
  68.4 4.8 %collective-permute-start.4 = (f32[5,2,16,128]{3,2,1,0:T(8,128)S(1)}, f32[5,2,16,128]{3,2,1,0:T(8,128)S(1)}, u32[]{:S(2)}, u32[]{:S(2)}) collective-permute-start(f32[5,2,16,128]{3,2,1,0:T(8,128)S(1)} %get-tuple-element.76), channel_id=1, source_target_pairs={{0,1},{1,2},{2,3},{4,5},{5,6},{6,7},{8,9},{9,10},{10,11},{12,13},{... | collective-permute-start | bytes 245768 | tf_op jit(solution)/shard_map/ppermute | solution.py:22
  73.2 1.3 collective-permute-start.5
  74.8 0.4 fusion.30
  75.3 4.3 %collective-permute-done.5 = f32[5,2,16,128]{3,2,1,0:T(8,128)S(1)} collective-permute-done((f32[5,2,16,128]{3,2,1,0:T(8,128)S(1)}, f32[5,2,16,128]{3,2,1,0:T(8,128)S(1)}, u32[]{:S(2)}, u32[]{:S(2)}) %collective-permute-start.5) | collective-permute-done | bytes 81952 | tf_op jit(solution)/shard_map/ppermute | solution.py:25
  79.8 0.1 fusion.63
  79.9 0.2 fusion.88
  80.1 0.4 slice_reduce_fusion
  80.6 0.1 reshape.109
  80.7 0.1 reshape.110
  80.9 0.3 pad_maximum_fusion.9
  81.4 1.1 fusion.2
  82.5 5.2 %collective-permute-start.10 = (f32[5,8,2,128]{3,2,1,0:T(2,128)S(1)}, f32[5,8,2,128]{3,2,1,0:T(2,128)S(1)}, u32[]{:S(2)}, u32[]{:S(2)}) collective-permute-start(f32[5,8,2,128]{3,2,1,0:T(2,128)S(1)} %get-tuple-element.74), channel_id=1, source_target_pairs={{0,4},{4,8},{8,12},{12,16},{16,20},{20,24},{24,28},{1,5},{5,9},{9,... | collective-permute-start | bytes 122888 | tf_op jit(solution)/shard_map/ppermute | solution.py:22
  87.7 1.3 collective-permute-start.11
  89.0 2.3 %collective-permute-start.8 = (f32[5,2,16,128]{3,2,1,0:T(8,128)S(1)}, f32[5,2,16,128]{3,2,1,0:T(8,128)S(1)}, u32[]{:S(2)}, u32[]{:S(2)}) collective-permute-start(f32[5,2,16,128]{3,2,1,0:T(8,128)S(1)} %get-tuple-element.70), channel_id=1, source_target_pairs={{0,1},{1,2},{2,3},{4,5},{5,6},{6,7},{8,9},{9,10},{10,11},{12,13},{... | collective-permute-start | bytes 245768 | tf_op jit(solution)/shard_map/ppermute | solution.py:22
  91.3 1.5 collective-permute-start.9
  92.8 1.4 collective-permute-done.11
  94.5 0.4 fusion.23
  94.9 2.8 %collective-permute-done.9 = f32[5,2,16,128]{3,2,1,0:T(8,128)S(1)} collective-permute-done((f32[5,2,16,128]{3,2,1,0:T(8,128)S(1)}, f32[5,2,16,128]{3,2,1,0:T(8,128)S(1)}, u32[]{:S(2)}, u32[]{:S(2)}) %collective-permute-start.9) | collective-permute-done | bytes 81952 | tf_op jit(solution)/shard_map/ppermute | solution.py:25
  98.0 0.3 fusion.83
  98.3 0.7 slice_select_fusion.1
  99.1 0.6 dynamic-slice
  100.3 39.2 %all-reduce.5.cloned.1.call-done = (f32[10,16,128]{2,1,0:T(8,128)}, f32[10,16,128]{2,1,0:T(8,128)}) async-done(((f32[10,16,128]{2,1,0:T(8,128)}, f32[10,16,128]{2,1,0:T(8,128)}), (f32[10,16,128]{2,1,0:T(8,128)}, f32[10,16,128]{2,1,0:T(8,128)})) %all-reduce.5.cloned.1.call-update) | async-done | bytes 163856
  139.4 0.8 dynamic-slice_multiply_fusion.1
  140.2 0.8 dynamic-slice_multiply_fusion
  141.0 0.9 add_reduce_fusion.1
  142.0 0.8 add_bitcast_fusion.1
  142.8 0.2 maximum_bitcast_fusion.1
  143.0 0.2 maximum_bitcast_fusion
  143.3 1.8 %pad_maximum_fusion = f32[2,49,10,4,128]{4,3,2,1,0:T(4,128)} fusion(f32[1,49,10,4,128]{4,3,2,1,0:T(4,128)S(1)} %maximum_bitcast_fusion.1, f32[1,49,10,4,128]{4,3,2,1,0:T(4,128)S(1)} %maximum_bitcast_fusion), kind=kLoop, calls=%fused_computation | loop fusion | flops 501760 | bytes 4014080 | tf_op jit(solution)/shard_map/stack | solution.py:169
  145.0 0.6 pad_maximum_fusion.28
  (99 shorter events, 2.2 us)
Async XLA Ops:
  7.2 17.6 %copy-start = (f32[5,8,16,128]{3,2,1,0:T(8,128)S(1)}, f32[5,8,16,128]{3,2,1,0:T(8,128)}, u32[]{:S(2)}) copy-start(f32[5,8,16,128]{3,2,1,0:T(8,128)} %param.5) | copy-start | bytes 983044
  7.2 132.3 %all-reduce.5.cloned.1.call-start = ((), (), s32[]{:S(2)}) async-start(), calls=%async_computation | async-start | bytes 327680
  8.9 50.1 %collective-permute-start.2 = (f32[5,8,2,128]{3,2,1,0:T(2,128)}, f32[5,8,2,128]{3,2,1,0:T(2,128)}, u32[]{:S(2)}, u32[]{:S(2)}) collective-permute-start(f32[5,8,2,128]{3,2,1,0:T(2,128)} %get-tuple-element.86), channel_id=1, source_target_pairs={{0,4},{4,8},{8,12},{12,16},{16,20},{20,24},{24,28},{1,5},{5,9},{9,... | collective-permute-start | bytes 122888 | tf_op jit(solution)/shard_map/ppermute | solution.py:22
  11.9 47.8 %collective-permute-start.3 = (f32[5,8,2,128]{3,2,1,0:T(2,128)}, f32[5,8,2,128]{3,2,1,0:T(2,128)}, u32[]{:S(2)}, u32[]{:S(2)}) collective-permute-start(f32[5,8,2,128]{3,2,1,0:T(2,128)} %get-tuple-element.85), channel_id=1, source_target_pairs={{4,0},{8,4},{12,8},{16,12},{20,16},{24,20},{28,24},{5,1},{9,5},{13... | collective-permute-start | bytes 122888 | tf_op jit(solution)/shard_map/ppermute | solution.py:25
  14.8 46.4 %collective-permute-start = (f32[5,2,16,128]{3,2,1,0:T(8,128)}, f32[5,2,16,128]{3,2,1,0:T(8,128)}, u32[]{:S(2)}, u32[]{:S(2)}) collective-permute-start(f32[5,2,16,128]{3,2,1,0:T(8,128)} %get-tuple-element.82), channel_id=1, source_target_pairs={{0,1},{1,2},{2,3},{4,5},{5,6},{6,7},{8,9},{9,10},{10,11},{12,13},{... | collective-permute-start | bytes 245768 | tf_op jit(solution)/shard_map/ppermute | solution.py:22
  19.7 41.5 %collective-permute-start.1 = (f32[5,2,16,128]{3,2,1,0:T(8,128)}, f32[5,2,16,128]{3,2,1,0:T(8,128)}, u32[]{:S(2)}, u32[]{:S(2)}) collective-permute-start(f32[5,2,16,128]{3,2,1,0:T(8,128)} %get-tuple-element.81), channel_id=1, source_target_pairs={{1,0},{2,1},{3,2},{5,4},{6,5},{7,6},{9,8},{10,9},{11,10},{13,12},{... | collective-permute-start | bytes 245768 | tf_op jit(solution)/shard_map/ppermute | solution.py:25
  25.2 1.2 copy-start.5
  25.3 1.2 copy-start.6
  25.3 4.1 %copy-start.1 = (f32[2,49,10,4,128]{4,3,2,1,0:T(4,128)S(1)}, f32[2,49,10,4,128]{4,3,2,1,0:T(4,128)}, u32[]{:S(2)}) copy-start(f32[2,49,10,4,128]{4,3,2,1,0:T(4,128)} %param.7) | copy-start | bytes 6021124
  62.2 1.0 copy-start.2
  65.8 8.8 %collective-permute-start.6 = (f32[5,8,2,128]{3,2,1,0:T(2,128)S(1)}, f32[5,8,2,128]{3,2,1,0:T(2,128)S(1)}, u32[]{:S(2)}, u32[]{:S(2)}) collective-permute-start(f32[5,8,2,128]{3,2,1,0:T(2,128)S(1)} %get-tuple-element.80), channel_id=1, source_target_pairs={{0,4},{4,8},{8,12},{12,16},{16,20},{20,24},{24,28},{1,5},{5,9},{9,... | collective-permute-start | bytes 122888 | tf_op jit(solution)/shard_map/ppermute | solution.py:22
  67.1 7.5 %collective-permute-start.7 = (f32[5,8,2,128]{3,2,1,0:T(2,128)S(1)}, f32[5,8,2,128]{3,2,1,0:T(2,128)S(1)}, u32[]{:S(2)}, u32[]{:S(2)}) collective-permute-start(f32[5,8,2,128]{3,2,1,0:T(2,128)S(1)} %get-tuple-element.79), channel_id=1, source_target_pairs={{4,0},{8,4},{12,8},{16,12},{20,16},{24,20},{28,24},{5,1},{9,5},{13... | collective-permute-start | bytes 122888 | tf_op jit(solution)/shard_map/ppermute | solution.py:25
  68.4 6.9 %collective-permute-start.4 = (f32[5,2,16,128]{3,2,1,0:T(8,128)S(1)}, f32[5,2,16,128]{3,2,1,0:T(8,128)S(1)}, u32[]{:S(2)}, u32[]{:S(2)}) collective-permute-start(f32[5,2,16,128]{3,2,1,0:T(8,128)S(1)} %get-tuple-element.76), channel_id=1, source_target_pairs={{0,1},{1,2},{2,3},{4,5},{5,6},{6,7},{8,9},{9,10},{10,11},{12,13},{... | collective-permute-start | bytes 245768 | tf_op jit(solution)/shard_map/ppermute | solution.py:22
  73.2 6.3 %collective-permute-start.5 = (f32[5,2,16,128]{3,2,1,0:T(8,128)S(1)}, f32[5,2,16,128]{3,2,1,0:T(8,128)S(1)}, u32[]{:S(2)}, u32[]{:S(2)}) collective-permute-start(f32[5,2,16,128]{3,2,1,0:T(8,128)S(1)} %get-tuple-element.75), channel_id=1, source_target_pairs={{1,0},{2,1},{3,2},{5,4},{6,5},{7,6},{9,8},{10,9},{11,10},{13,12},{... | collective-permute-start | bytes 245768 | tf_op jit(solution)/shard_map/ppermute | solution.py:25
  82.5 10.3 %collective-permute-start.10 = (f32[5,8,2,128]{3,2,1,0:T(2,128)S(1)}, f32[5,8,2,128]{3,2,1,0:T(2,128)S(1)}, u32[]{:S(2)}, u32[]{:S(2)}) collective-permute-start(f32[5,8,2,128]{3,2,1,0:T(2,128)S(1)} %get-tuple-element.74), channel_id=1, source_target_pairs={{0,4},{4,8},{8,12},{12,16},{16,20},{20,24},{24,28},{1,5},{5,9},{9,... | collective-permute-start | bytes 122888 | tf_op jit(solution)/shard_map/ppermute | solution.py:22
  87.7 6.5 %collective-permute-start.11 = (f32[5,8,2,128]{3,2,1,0:T(2,128)S(1)}, f32[5,8,2,128]{3,2,1,0:T(2,128)S(1)}, u32[]{:S(2)}, u32[]{:S(2)}) collective-permute-start(f32[5,8,2,128]{3,2,1,0:T(2,128)S(1)} %get-tuple-element.73), channel_id=1, source_target_pairs={{4,0},{8,4},{12,8},{16,12},{20,16},{24,20},{28,24},{5,1},{9,5},{13... | collective-permute-start | bytes 122888 | tf_op jit(solution)/shard_map/ppermute | solution.py:25
  89.0 5.8 %collective-permute-start.8 = (f32[5,2,16,128]{3,2,1,0:T(8,128)S(1)}, f32[5,2,16,128]{3,2,1,0:T(8,128)S(1)}, u32[]{:S(2)}, u32[]{:S(2)}) collective-permute-start(f32[5,2,16,128]{3,2,1,0:T(8,128)S(1)} %get-tuple-element.70), channel_id=1, source_target_pairs={{0,1},{1,2},{2,3},{4,5},{5,6},{6,7},{8,9},{9,10},{10,11},{12,13},{... | collective-permute-start | bytes 245768 | tf_op jit(solution)/shard_map/ppermute | solution.py:22
  91.3 6.3 %collective-permute-start.9 = (f32[5,2,16,128]{3,2,1,0:T(8,128)S(1)}, f32[5,2,16,128]{3,2,1,0:T(8,128)S(1)}, u32[]{:S(2)}, u32[]{:S(2)}) collective-permute-start(f32[5,2,16,128]{3,2,1,0:T(8,128)S(1)} %get-tuple-element.69), channel_id=1, source_target_pairs={{1,0},{2,1},{3,2},{5,4},{6,5},{7,6},{9,8},{10,9},{11,10},{13,12},{... | collective-permute-start | bytes 245768 | tf_op jit(solution)/shard_map/ppermute | solution.py:25
  98.0 1.1 copy-start.7
  98.0 43.0 %copy-start.4 = (f32[24,4,128]{2,1,0:T(4,128)S(1)}, f32[24,4,128]{2,1,0:T(4,128)}, u32[]{:S(2)}) copy-start(f32[24,4,128]{2,1,0:T(4,128)} %get-tuple-element.124) | copy-start | bytes 147460
  98.3 43.7 %copy-start.3 = (f32[5,8,16,128]{3,2,1,0:T(8,128)}, f32[5,8,16,128]{3,2,1,0:T(8,128)S(1)}, u32[]{:S(2)}) copy-start(f32[5,8,16,128]{3,2,1,0:T(8,128)S(1)} %fusion.83) | copy-start | bytes 983044
Sparse Core Ops, SparseCore 0:
  99.2 40.2 all-reduce.4
where the time goes:
time: 153 us; the launch traced here: 152 us
  waiting for transfers between devices  47.7 us (31%)
  starting transfers between devices  29.4 us (19%)
  blocking collectives  27.7 us (18%)
  other arithmetic  21.4 us (14%)
  between operations  15.5 us (10%)
  local copies, waits for them, and re-layouts  10.7 us (7%)
    unnamed x2, waiting for transfers between devices  39.2 us
    ppermute x6, starting transfers between devices, padded_2(): lax.ppermute(lax.slice_in_dim(block, block.shape[dim] - width, None, axis...  21.5 us
    all_gather x1, blocking collectives, shards(): lax.all_gather(low_share, 'pitch', axis=1, tiled=True)  14.3 us
    all_gather x1, blocking collectives, shards(): lax.all_gather(high_share, 'pitch', axis=1, tiled=True)  13.3 us
    ppermute x6, waiting for transfers between devices, padded_2(): lax.ppermute(lax.slice_in_dim(block, 0, width, axis=dim), axis, backward)  8.44 us
    ppermute x6, starting transfers between devices, padded_2(): lax.ppermute(lax.slice_in_dim(block, 0, width, axis=dim), axis, backward)  7.91 us
    sub x9, other arithmetic, face_sum(): 0.5 * (window(cell_flux, 1, faces_n) + window(cell_flux, 2, faces_n))  4.7 us
    slice x6, local copies, waits for them, and re-layouts, padded_2(): lax.slice_in_dim(block, 0, width, axis=dim)  3.38 us
  transfers between devices with their start and end apart: 13, of which 5 were waited for; matrix products, arithmetic and copies ran while one was open for 10% of the time, Pallas kernels for 0%

commit v1 on v0

--- a/solution.py
+++ b/solution.py
@@ -109,9 +109,33 @@
     phases = sample_times.astype(jnp.float32) * period
     low_share = rebuild(fourier_store[0], phases[0] - phase_lag, harmonics)
     high_share = rebuild(fourier_store[1], phases[1] + phase_lag, harmonics)
+
+    def hold_trails(frame):
+        x_new, x_next, outer = (
+            lax.psum(1, axis_name="pitch"),
+            lax.axis_index("pitch"),
+            frame.shape[1],
+        )
+        series = tuple(
+            (dev_i * x_new if hop_no == 1 else dev_i for hop_no, dev_i in enumerate(frame.shape))
+        )
+        after = lax.dynamic_update_slice_in_dim(
+            jnp.zeros(series, frame.dtype), frame, x_next * outer, axis=1
+        )
+        for k0 in tuple(range(1, x_new)):
+            frame = lax.ppermute(
+                frame,
+                axis_name="pitch",
+                perm=tuple(((hop_no, (hop_no + 1) % x_new) for hop_no in range(x_new))),
+            )
+            after = lax.dynamic_update_slice_in_dim(
+                after, frame, (x_next - k0) % x_new * outer, axis=1
+            )
+        return after
+
     low_whole, high_whole = (
         lax.all_gather(low_share, "pitch", axis=1, tiled=True),
-        lax.all_gather(high_share, "pitch", axis=1, tiled=True),
+        hold_trails(high_share),
     )
     ghost_shape = (5, 2, block_rows, radial_cells)
     low_ghost = low_whole.reshape(ghost_shape)

time: 153 us -> 146 us (0.954)
  blocking collectives: 27.7 us -> 14.9 us
  waiting for transfers between devices: 47.7 us -> 54.5 us
  other arithmetic: 21.4 us -> 23.6 us
  local copies, waits for them, and re-layouts: 10.7 us -> 8.8 us
  starting transfers between devices: 29.4 us -> 27.5 us
    all_gather x1 -> x0, blocking collectives: 13.3 us -> none  [shards(): lax.all_gather(high_share, 'pitch', axis=1, tiled=True)]
    ppermute x0 -> x3, waiting for transfers between devices: none -> 7.97 us  [hold_trails(): lax.ppermute(frame, axis_name='pitch', perm=tuple(((hop_no, (hop_no + 1)...]
    ppermute x6, starting transfers between devices: 21.5 us -> 18.1 us  [padded_2(): lax.ppermute(lax.slice_in_dim(block, block.shape[dim] - width, None, axis...]
  transfers between devices with their start and end apart: 13 -> 16, of which waited for: 5 -> 7; matrix products, arithmetic and copies ran while one was open for 10% -> 11% of each run, Pallas kernels for 0% -> 0%
where the time goes in v1:
time: 146 us; the launch traced here: 145 us
  waiting for transfers between devices  54.5 us (37%)
  starting transfers between devices  27.5 us (19%)
  other arithmetic  23.6 us (16%)
  between operations  15.5 us (11%)
  blocking collectives  14.9 us (10%)
  local copies, waits for them, and re-layouts  8.8 us (6%)
    unnamed x2, waiting for transfers between devices  38.1 us
    ppermute x6, starting transfers between devices, padded_2(): lax.ppermute(lax.slice_in_dim(block, block.shape[dim] - width, None, axis...  18.1 us
    all_gather x1, blocking collectives, shards(): lax.all_gather(low_share, 'pitch', axis=1, tiled=True)  14.9 us
    ppermute x6, waiting for transfers between devices, padded_2(): lax.ppermute(lax.slice_in_dim(block, 0, width, axis=dim), axis, backward)  8.49 us
    ppermute x3, waiting for transfers between devices, hold_trails(): lax.ppermute(frame, axis_name='pitch', perm=tuple(((hop_no, (hop_no + 1)...  7.97 us
    ppermute x6, starting transfers between devices, padded_2(): lax.ppermute(lax.slice_in_dim(block, 0, width, axis=dim), axis, backward)  7.91 us
    sub x9, other arithmetic, face_sum(): 0.5 * (window(cell_flux, 1, faces_n) + window(cell_flux, 2, faces_n))  4.71 us
    slice x6, local copies, waits for them, and re-layouts, padded_2(): lax.slice_in_dim(block, 0, width, axis=dim)  3.5 us
  transfers between devices with their start and end apart: 16, of which 7 were waited for; matrix products, arithmetic and copies ran while one was open for 11% of the time, Pallas kernels for 0%

profile of v1, /device:TPU:0, one launch (start us, length us, event | category | flops | bytes accessed | tf_op | source)
XLA Modules:
  0.0 144.9 jit_solution(6735472753304272070)
XLA Ops:
  7.2 1.8 %fusion.114 = (f32[5,8,2,128]{3,2,1,0:T(2,128)}, f32[5,8,2,128]{3,2,1,0:T(2,128)}) fusion(f32[5,8,16,128]{3,2,1,0:T(8,128)} %param.5), kind=kLoop, calls=%fused_computation.309 | loop fusion | bytes 163840 | tf_op jit(solution)/shard_map/slice | solution.py:25
  9.0 3.0 %collective-permute-start.5 = (f32[5,8,2,128]{3,2,1,0:T(2,128)}, f32[5,8,2,128]{3,2,1,0:T(2,128)}, u32[]{:S(2)}, u32[]{:S(2)}) collective-permute-start(f32[5,8,2,128]{3,2,1,0:T(2,128)} %get-tuple-element.84), channel_id=1, source_target_pairs={{0,4},{4,8},{8,12},{12,16},{16,20},{20,24},{24,28},{1,5},{5,9},{9,... | collective-permute-start | bytes 122888 | tf_op jit(solution)/shard_map/ppermute | solution.py:22
  12.0 1.3 collective-permute-start.6
  13.3 1.6 %fusion.112 = (f32[5,2,16,128]{3,2,1,0:T(8,128)}, f32[5,2,16,128]{3,2,1,0:T(8,128)}) fusion(f32[5,8,16,128]{3,2,1,0:T(8,128)} %param.5), kind=kLoop, calls=%fused_computation.307 | loop fusion | bytes 327680 | tf_op jit(solution)/shard_map/slice | solution.py:25
  14.9 4.9 %collective-permute-start = (f32[5,2,16,128]{3,2,1,0:T(8,128)}, f32[5,2,16,128]{3,2,1,0:T(8,128)}, u32[]{:S(2)}, u32[]{:S(2)}) collective-permute-start(f32[5,2,16,128]{3,2,1,0:T(8,128)} %get-tuple-element.80), channel_id=1, source_target_pairs={{0,1},{1,2},{2,3},{4,5},{5,6},{6,7},{8,9},{9,10},{10,11},{12,13},{... | collective-permute-start | bytes 245768 | tf_op jit(solution)/shard_map/ppermute | solution.py:22
  19.9 0.7 broadcast_add_fusion
  20.5 2.9 %multiply_sine_fusion.3 = (f32[24,4,128]{2,1,0:T(4,128)S(1)}, f32[24,4,128]{2,1,0:T(4,128)S(1)}, f32[24,4,128]{2,1,0:T(4,128)S(1)}, f32[24,4,128]{2,1,0:T(4,128)...) fusion(f32[4,128]{1,0:T(4,128)S(1)} %get-tuple-element.126, ...), kind=kLoop, calls=%fused_computation.246 | loop fusion | flops 184320 | bytes 604352 | tf_op jit(solution)/shard_map/sin | solution.py:72
  23.5 1.9 %fusion.43 = (f32[10,4,128]{2,1,0:T(4,128)S(1)}, f32[10,4,128]{2,1,0:T(4,128)S(1)}) fusion(f32[2,49,10,4,128]{4,3,2,1,0:T(4,128)} %param.7, f32[24,4,128]{2,1,0:T(4,128)S(1)} %get-tuple-element.118, f32[24,4,128]{2,1,0:T(4,128)S(1)} %get-tuple-element.117, f32[24,4,128]{2,1,0:T(4,128)S(1)} %get-tuple-element.114, f32[24,4,128]{2,1,0:T(4,128)S(1)} %get-tuple-element.113), kind=kLoop, calls=%fused_computation.81 | loop fusion | flops 972800 | bytes 2203648 | tf_op jit(solution)/shard_map/reduce_sum | solution.py:84
  25.4 0.6 constant_dynamic-update-slice_fusion.9
  26.1 1.0 collective-permute-start.1
  27.1 1.3 collective-permute-start.4
  28.3 0.2 fusion.115
  28.5 0.6 fusion.113
  29.2 0.3 copy.52
  29.4 0.3 copy.53
  29.7 0.2 reshape.105
  29.9 0.1 reshape.106
  30.1 0.3 pad_maximum_fusion.7
  30.6 1.1 fusion.16
  31.7 14.9 %all_gather.3 = f32[10,16,128]{2,0,1:T(8,128)S(1)} all-gather(f32[10,4,128]{2,0,1:T(8,128)S(1)} %copy.44), channel_id=1, replica_groups=mesh['blk'=8,'pitch'=4] {'pitch'}, dimensions={1}, use_global_device_ids=true | all-gather | bytes 102400 | tf_op jit(solution)/shard_map/all_gather | solution.py:137
  46.7 0.5 collective-permute-start.2
  47.2 0.8 constant_dynamic-update-slice_fusion.8
  48.0 0.8 broadcast_select_fusion.5
  48.7 0.8 broadcast_select_fusion.2
  49.8 0.4 fusion.37
  50.2 2.4 %collective-permute-done.2 = f32[10,4,128]{2,1,0:T(4,128)S(1)} collective-permute-done((f32[10,4,128]{2,1,0:T(4,128)}, f32[10,4,128]{2,1,0:T(4,128)S(1)}, u32[]{:S(2)}, u32[]{:S(2)}) %collective-permute-start.2) | collective-permute-done | bytes 20512 | tf_op jit(solution)/shard_map/ppermute | solution.py:126
  52.6 5.6 %collective-permute-done.3 = f32[10,4,128]{2,1,0:T(4,128)S(1)} collective-permute-done((f32[10,4,128]{2,1,0:T(4,128)S(1)}, f32[10,4,128]{2,1,0:T(4,128)S(1)}, u32[]{:S(2)}, u32[]{:S(2)}) %collective-permute-start.3) | collective-permute-done | bytes 20512 | tf_op jit(solution)/shard_map/ppermute | solution.py:126
  58.2 0.9 broadcast_select_fusion.8
  59.4 0.7 copy-done.2
  60.1 0.3 fusion.93
  60.4 0.4 slice_reduce_fusion.2
  61.0 0.1 reshape.108
  61.1 0.3 pad_maximum_fusion.8
  61.6 1.1 fusion.9
  62.7 1.3 collective-permute-start.9
  64.1 1.3 collective-permute-start.10
  65.4 1.3 collective-permute-start.7
  66.7 1.3 collective-permute-start.8
  68.0 2.5 %collective-permute-done.10 = f32[5,8,2,128]{3,2,1,0:T(2,128)S(1)} collective-permute-done((f32[5,8,2,128]{3,2,1,0:T(2,128)S(1)}, f32[5,8,2,128]{3,2,1,0:T(2,128)S(1)}, u32[]{:S(2)}, u32[]{:S(2)}) %collective-permute-start.10) | collective-permute-done | bytes 40992 | tf_op jit(solution)/shard_map/ppermute | solution.py:25
  70.8 0.4 fusion.30
  71.2 1.8 %collective-permute-done.8 = f32[5,2,16,128]{3,2,1,0:T(8,128)S(1)} collective-permute-done((f32[5,2,16,128]{3,2,1,0:T(8,128)S(1)}, f32[5,2,16,128]{3,2,1,0:T(8,128)S(1)}, u32[]{:S(2)}, u32[]{:S(2)}) %collective-permute-start.8) | collective-permute-done | bytes 81952 | tf_op jit(solution)/shard_map/ppermute | solution.py:25
  73.3 0.2 fusion.88
  73.6 0.4 slice_reduce_fusion
  74.3 0.3 pad_maximum_fusion.9
  74.9 1.1 fusion.2
  75.9 5.2 %collective-permute-start.13 = (f32[5,8,2,128]{3,2,1,0:T(2,128)S(1)}, f32[5,8,2,128]{3,2,1,0:T(2,128)S(1)}, u32[]{:S(2)}, u32[]{:S(2)}) collective-permute-start(f32[5,8,2,128]{3,2,1,0:T(2,128)S(1)} %get-tuple-element.72), channel_id=1, source_target_pairs={{0,4},{4,8},{8,12},{12,16},{16,20},{20,24},{24,28},{1,5},{5,9},{9,... | collective-permute-start | bytes 122888 | tf_op jit(solution)/shard_map/ppermute | solution.py:22
  81.2 1.3 collective-permute-start.14
  82.5 2.4 %collective-permute-start.11 = (f32[5,2,16,128]{3,2,1,0:T(8,128)S(1)}, f32[5,2,16,128]{3,2,1,0:T(8,128)S(1)}, u32[]{:S(2)}, u32[]{:S(2)}) collective-permute-start(f32[5,2,16,128]{3,2,1,0:T(8,128)S(1)} %get-tuple-element.68), channel_id=1, source_target_pairs={{0,1},{1,2},{2,3},{4,5},{5,6},{6,7},{8,9},{9,10},{10,11},{12,13},{... | collective-permute-start | bytes 245768 | tf_op jit(solution)/shard_map/ppermute | solution.py:22
  84.9 1.5 %collective-permute-start.12 = (f32[5,2,16,128]{3,2,1,0:T(8,128)S(1)}, f32[5,2,16,128]{3,2,1,0:T(8,128)S(1)}, u32[]{:S(2)}, u32[]{:S(2)}) collective-permute-start(f32[5,2,16,128]{3,2,1,0:T(8,128)S(1)} %get-tuple-element.67), channel_id=1, source_target_pairs={{1,0},{2,1},{3,2},{5,4},{6,5},{7,6},{9,8},{10,9},{11,10},{13,12},{... | collective-permute-start | bytes 245768 | tf_op jit(solution)/shard_map/ppermute | solution.py:25
  86.4 1.2 collective-permute-done.14
  87.8 0.4 fusion.23
  88.2 3.0 %collective-permute-done.12 = f32[5,2,16,128]{3,2,1,0:T(8,128)S(1)} collective-permute-done((f32[5,2,16,128]{3,2,1,0:T(8,128)S(1)}, f32[5,2,16,128]{3,2,1,0:T(8,128)S(1)}, u32[]{:S(2)}, u32[]{:S(2)}) %collective-permute-start.12) | collective-permute-done | bytes 81952 | tf_op jit(solution)/shard_map/ppermute | solution.py:25
  91.6 0.2 fusion.83
  91.8 0.7 slice_select_fusion.1
  92.6 0.6 dynamic-slice
  93.8 38.1 %all-reduce.5.cloned.1.call-done = (f32[10,16,128]{2,1,0:T(8,128)}, f32[10,16,128]{2,1,0:T(8,128)}) async-done(((f32[10,16,128]{2,1,0:T(8,128)}, f32[10,16,128]{2,1,0:T(8,128)}), (f32[10,16,128]{2,1,0:T(8,128)}, f32[10,16,128]{2,1,0:T(8,128)})) %all-reduce.5.cloned.1.call-update) | async-done | bytes 163856
  131.9 0.8 dynamic-slice_multiply_fusion.1
  132.7 0.8 dynamic-slice_multiply_fusion
  133.5 0.9 add_reduce_fusion.1
  134.4 0.8 add_bitcast_fusion.1
  135.2 0.2 maximum_bitcast_fusion.1
  135.5 0.2 maximum_bitcast_fusion
  135.7 1.8 %pad_maximum_fusion = f32[2,49,10,4,128]{4,3,2,1,0:T(4,128)} fusion(f32[1,49,10,4,128]{4,3,2,1,0:T(4,128)S(1)} %maximum_bitcast_fusion.1, f32[1,49,10,4,128]{4,3,2,1,0:T(4,128)S(1)} %maximum_bitcast_fusion), kind=kLoop, calls=%fused_computation | loop fusion | flops 501760 | bytes 4014080 | tf_op jit(solution)/shard_map/stack | solution.py:193
  137.4 0.6 pad_maximum_fusion.28
  (100 shorter events, 2.8 us)
Async XLA Ops:
  7.2 21.2 %copy-start = (f32[5,8,16,128]{3,2,1,0:T(8,128)S(1)}, f32[5,8,16,128]{3,2,1,0:T(8,128)}, u32[]{:S(2)}) copy-start(f32[5,8,16,128]{3,2,1,0:T(8,128)} %param.5) | copy-start | bytes 983044
  7.2 18.3 %copy-start.1 = (f32[2,49,10,4,128]{4,3,2,1,0:T(4,128)S(1)}, f32[2,49,10,4,128]{4,3,2,1,0:T(4,128)}, u32[]{:S(2)}) copy-start(f32[2,49,10,4,128]{4,3,2,1,0:T(4,128)} %param.7) | copy-start | bytes 6021124
  7.2 124.7 %all-reduce.5.cloned.1.call-start = ((), (), s32[]{:S(2)}) async-start(), calls=%async_computation | async-start | bytes 327680
  9.0 38.9 %collective-permute-start.5 = (f32[5,8,2,128]{3,2,1,0:T(2,128)}, f32[5,8,2,128]{3,2,1,0:T(2,128)}, u32[]{:S(2)}, u32[]{:S(2)}) collective-permute-start(f32[5,8,2,128]{3,2,1,0:T(2,128)} %get-tuple-element.84), channel_id=1, source_target_pairs={{0,4},{4,8},{8,12},{12,16},{16,20},{20,24},{24,28},{1,5},{5,9},{9,... | collective-permute-start | bytes 122888 | tf_op jit(solution)/shard_map/ppermute | solution.py:22
  12.0 36.7 %collective-permute-start.6 = (f32[5,8,2,128]{3,2,1,0:T(2,128)}, f32[5,8,2,128]{3,2,1,0:T(2,128)}, u32[]{:S(2)}, u32[]{:S(2)}) collective-permute-start(f32[5,8,2,128]{3,2,1,0:T(2,128)} %get-tuple-element.83), channel_id=1, source_target_pairs={{4,0},{8,4},{12,8},{16,12},{20,16},{24,20},{28,24},{5,1},{9,5},{13... | collective-permute-start | bytes 122888 | tf_op jit(solution)/shard_map/ppermute | solution.py:25
  14.9 43.2 %collective-permute-start = (f32[5,2,16,128]{3,2,1,0:T(8,128)}, f32[5,2,16,128]{3,2,1,0:T(8,128)}, u32[]{:S(2)}, u32[]{:S(2)}) collective-permute-start(f32[5,2,16,128]{3,2,1,0:T(8,128)} %get-tuple-element.80), channel_id=1, source_target_pairs={{0,1},{1,2},{2,3},{4,5},{5,6},{6,7},{8,9},{9,10},{10,11},{12,13},{... | collective-permute-start | bytes 245768 | tf_op jit(solution)/shard_map/ppermute | solution.py:22
  26.1 20.6 %collective-permute-start.1 = (f32[10,4,128]{2,1,0:T(4,128)}, f32[10,4,128]{2,1,0:T(4,128)}, u32[]{:S(2)}, u32[]{:S(2)}) collective-permute-start(f32[10,4,128]{2,1,0:T(4,128)} %get-tuple-element.46), channel_id=1, source_target_pairs={{0,1},{1,2},{2,3},{3,0},{4,5},{5,6},{6,7},{7,4},{8,9},{9,10},{10,1... | collective-permute-start | bytes 61448 | tf_op jit(solution)/shard_map/ppermute | solution.py:126
  27.1 31.1 %collective-permute-start.4 = (f32[5,2,16,128]{3,2,1,0:T(8,128)}, f32[5,2,16,128]{3,2,1,0:T(8,128)}, u32[]{:S(2)}, u32[]{:S(2)}) collective-permute-start(f32[5,2,16,128]{3,2,1,0:T(8,128)} %get-tuple-element.79), channel_id=1, source_target_pairs={{1,0},{2,1},{3,2},{5,4},{6,5},{7,6},{9,8},{10,9},{11,10},{13,12},{... | collective-permute-start | bytes 245768 | tf_op jit(solution)/shard_map/ppermute | solution.py:25
  46.7 5.8 %collective-permute-start.2 = (f32[10,4,128]{2,1,0:T(4,128)}, f32[10,4,128]{2,1,0:T(4,128)S(1)}, u32[]{:S(2)}, u32[]{:S(2)}) collective-permute-start(f32[10,4,128]{2,1,0:T(4,128)} %collective-permute-done.1), channel_id=1, source_target_pairs={{0,1},{1,2},{2,3},{3,0},{4,5},{5,6},{6,7},{7,4},{8,9},{9,10},{10,1... | collective-permute-start | bytes 61448 | tf_op jit(solution)/shard_map/ppermute | solution.py:126
  52.6 5.6 %collective-permute-start.3 = (f32[10,4,128]{2,1,0:T(4,128)S(1)}, f32[10,4,128]{2,1,0:T(4,128)S(1)}, u32[]{:S(2)}, u32[]{:S(2)}) collective-permute-start(f32[10,4,128]{2,1,0:T(4,128)S(1)} %collective-permute-done.2), channel_id=1, source_target_pairs={{0,1},{1,2},{2,3},{3,0},{4,5},{5,6},{6,7},{7,4},{8,9},{9,10},{10,1... | collective-permute-start | bytes 61448 | tf_op jit(solution)/shard_map/ppermute | solution.py:126
  59.2 1.0 copy-start.2
  62.7 5.2 %collective-permute-start.9 = (f32[5,8,2,128]{3,2,1,0:T(2,128)S(1)}, f32[5,8,2,128]{3,2,1,0:T(2,128)S(1)}, u32[]{:S(2)}, u32[]{:S(2)}) collective-permute-start(f32[5,8,2,128]{3,2,1,0:T(2,128)S(1)} %get-tuple-element.78), channel_id=1, source_target_pairs={{0,4},{4,8},{8,12},{12,16},{16,20},{20,24},{24,28},{1,5},{5,9},{9,... | collective-permute-start | bytes 122888 | tf_op jit(solution)/shard_map/ppermute | solution.py:22
  64.1 6.5 %collective-permute-start.10 = (f32[5,8,2,128]{3,2,1,0:T(2,128)S(1)}, f32[5,8,2,128]{3,2,1,0:T(2,128)S(1)}, u32[]{:S(2)}, u32[]{:S(2)}) collective-permute-start(f32[5,8,2,128]{3,2,1,0:T(2,128)S(1)} %get-tuple-element.77), channel_id=1, source_target_pairs={{4,0},{8,4},{12,8},{16,12},{20,16},{24,20},{28,24},{5,1},{9,5},{13... | collective-permute-start | bytes 122888 | tf_op jit(solution)/shard_map/ppermute | solution.py:25
  65.4 5.8 %collective-permute-start.7 = (f32[5,2,16,128]{3,2,1,0:T(8,128)S(1)}, f32[5,2,16,128]{3,2,1,0:T(8,128)S(1)}, u32[]{:S(2)}, u32[]{:S(2)}) collective-permute-start(f32[5,2,16,128]{3,2,1,0:T(8,128)S(1)} %get-tuple-element.74), channel_id=1, source_target_pairs={{0,1},{1,2},{2,3},{4,5},{5,6},{6,7},{8,9},{9,10},{10,11},{12,13},{... | collective-permute-start | bytes 245768 | tf_op jit(solution)/shard_map/ppermute | solution.py:22
  66.7 6.3 %collective-permute-start.8 = (f32[5,2,16,128]{3,2,1,0:T(8,128)S(1)}, f32[5,2,16,128]{3,2,1,0:T(8,128)S(1)}, u32[]{:S(2)}, u32[]{:S(2)}) collective-permute-start(f32[5,2,16,128]{3,2,1,0:T(8,128)S(1)} %get-tuple-element.73), channel_id=1, source_target_pairs={{1,0},{2,1},{3,2},{5,4},{6,5},{7,6},{9,8},{10,9},{11,10},{13,12},{... | collective-permute-start | bytes 245768 | tf_op jit(solution)/shard_map/ppermute | solution.py:25
  75.9 10.4 %collective-permute-start.13 = (f32[5,8,2,128]{3,2,1,0:T(2,128)S(1)}, f32[5,8,2,128]{3,2,1,0:T(2,128)S(1)}, u32[]{:S(2)}, u32[]{:S(2)}) collective-permute-start(f32[5,8,2,128]{3,2,1,0:T(2,128)S(1)} %get-tuple-element.72), channel_id=1, source_target_pairs={{0,4},{4,8},{8,12},{12,16},{16,20},{20,24},{24,28},{1,5},{5,9},{9,... | collective-permute-start | bytes 122888 | tf_op jit(solution)/shard_map/ppermute | solution.py:22
  81.2 6.4 %collective-permute-start.14 = (f32[5,8,2,128]{3,2,1,0:T(2,128)S(1)}, f32[5,8,2,128]{3,2,1,0:T(2,128)S(1)}, u32[]{:S(2)}, u32[]{:S(2)}) collective-permute-start(f32[5,8,2,128]{3,2,1,0:T(2,128)S(1)} %get-tuple-element.71), channel_id=1, source_target_pairs={{4,0},{8,4},{12,8},{16,12},{20,16},{24,20},{28,24},{5,1},{9,5},{13... | collective-permute-start | bytes 122888 | tf_op jit(solution)/shard_map/ppermute | solution.py:25
  82.5 5.7 %collective-permute-start.11 = (f32[5,2,16,128]{3,2,1,0:T(8,128)S(1)}, f32[5,2,16,128]{3,2,1,0:T(8,128)S(1)}, u32[]{:S(2)}, u32[]{:S(2)}) collective-permute-start(f32[5,2,16,128]{3,2,1,0:T(8,128)S(1)} %get-tuple-element.68), channel_id=1, source_target_pairs={{0,1},{1,2},{2,3},{4,5},{5,6},{6,7},{8,9},{9,10},{10,11},{12,13},{... | collective-permute-start | bytes 245768 | tf_op jit(solution)/shard_map/ppermute | solution.py:22
  84.9 6.3 %collective-permute-start.12 = (f32[5,2,16,128]{3,2,1,0:T(8,128)S(1)}, f32[5,2,16,128]{3,2,1,0:T(8,128)S(1)}, u32[]{:S(2)}, u32[]{:S(2)}) collective-permute-start(f32[5,2,16,128]{3,2,1,0:T(8,128)S(1)} %get-tuple-element.67), channel_id=1, source_target_pairs={{1,0},{2,1},{3,2},{5,4},{6,5},{7,6},{9,8},{10,9},{11,10},{13,12},{... | collective-permute-start | bytes 245768 | tf_op jit(solution)/shard_map/ppermute | solution.py:25
  91.6 1.0 copy-start.4
  91.8 42.6 %copy-start.3 = (f32[5,8,16,128]{3,2,1,0:T(8,128)}, f32[5,8,16,128]{3,2,1,0:T(8,128)S(1)}, u32[]{:S(2)}) copy-start(f32[5,8,16,128]{3,2,1,0:T(8,128)S(1)} %fusion.83) | copy-start | bytes 983044
Sparse Core Ops, SparseCore 0:
  92.7 39.1 all-reduce.4
